TPU v7x, 32 devices: a whole 2x2x4 slice. The times are simulated.
32 devices in a mesh: depth: 4 (over z), row: 8 (over y, x, core).
Axes of the slice: x: 2, y: 2, z: 4, core: 2. Of those that a mesh axis runs over, the one named last changes fastest.
Arguments:
- volume: float32 [192, 512, 2048], P('depth', 'row'), may hold values from -6 to 6
- transfer: float32 [8], replicated, may hold values from 0.3 to 1.2
Outputs:
- image: float32 [4, 512, 2048], P(None, 'row', 'depth')
All inputs are finite; a program needn't handle non-finite values.
Results may differ from a plain program's by a relative error of at most 0.0003.
Values sent between devices are 32-bit elements; how exact they have to be, the bound alone decides.
No kernel may reach another device: no remote copies, remote signals or barrier semaphores. Data moves between devices by JAX's collectives and lax.ppermute only.
A program may use at most 192 MiB of HBM per device.

v0:
```python
import functools
import math

import jax
import jax.numpy as jnp
from jax import lax
from jax.experimental import pallas as pl
from jax.experimental.pallas import tpu as pltpu
from jax.sharding import PartitionSpec as P


LANES = 128
SUBLANES = 8
LN2 = math.log(2.0)
SMEM = pl.BlockSpec(memory_space=pltpu.SMEM)
VMEM = pl.BlockSpec(memory_space=pltpu.VMEM)
ANY = pl.BlockSpec(memory_space=pl.ANY)


def by_parity(axis, even, odd):
    is_even = lax.rem(lax.axis_index(axis), 2) == 0
    pl.when(is_even)(even)
    pl.when(jnp.logical_not(is_even))(odd)


def start(*copies):
    for copy in copies:
        copy.start()


def cut_kernel(volume, slab_a, slab_b, strip_a, strip_b, sems):
    slices, rows, _ = volume.shape

    def slab(z, i):
        target = (slab_a, slab_b)[i]
        return pltpu.make_async_copy(volume.at[pl.ds(z, 1)], target, sems.at[i])

    def strip(y, i):
        target = (strip_a, strip_b)[i]
        return pltpu.make_async_copy(volume.at[:, pl.ds(y, 1), :], target, sems.at[2 + i])

    by_parity(
        "depth",
        lambda: start(slab(slices - 1, 0), slab(0, 1)),
        lambda: start(slab(0, 0), slab(slices - 1, 1)),
    )
    by_parity(
        "row",
        lambda: start(strip(rows - 1, 0), strip(0, 1)),
        lambda: start(strip(0, 0), strip(rows - 1, 1)),
    )
    for i in range(2):
        slab(0, i).wait()
        strip(0, i).wait()


def cut(volume):
    slices, rows, columns = volume.shape
    slab = jax.ShapeDtypeStruct((1, rows, columns), jnp.float32)
    strip = jax.ShapeDtypeStruct((slices, 1, columns), jnp.float32)
    return pl.pallas_call(
        cut_kernel,
        in_specs=[ANY],
        out_specs=[VMEM] * 4,
        out_shape=[slab, slab, strip, strip],
        scratch_shapes=[pltpu.SemaphoreType.DMA((4,))],
        name="cut",
    )(volume)


def swap(value, axis, first):
    pairs = []
    for i in range(first, lax.axis_size(axis) - 1, 2):
        pairs += [(i, i + 1), (i + 1, i)]
    return lax.ppermute(value, axis, pairs)


def tile_constants():
    lane = lax.broadcasted_iota(jnp.int32, (SUBLANES, LANES), 1)
    return lane == 0, lane == LANES - 1


def coefficients(transfer, slices):
    gamma = jnp.full((SUBLANES, LANES), transfer[6], jnp.float32) * (-2.0 / slices)
    ambient = 0.5 * jnp.full((SUBLANES, LANES), transfer[7], jnp.float32)
    return gamma, (1.0 - ambient) / (3.0 * ambient)


def cell(cells, c, z, row, x, below, above, state, coef, ends):
    log_t, passing, shade, tinted = state
    gamma, ratio = coef
    first, last = ends
    here = pl.ds(row, SUBLANES)
    right = cells[c + 1, z, here, :]
    left = cells[c - 1, z, here, :]
    d_row = cells[c, z, pl.ds(row + 1, SUBLANES), :] - cells[c, z, pl.ds(row - 1, SUBLANES), :]
    to_right = pltpu.roll(jnp.where(first, right, x), LANES - 1, 1)
    to_left = pltpu.roll(jnp.where(last, left, x), 1, 1)
    d_col = to_right - to_left
    d_depth = above - below
    plane = d_row + d_col
    along = d_depth + (plane + plane)
    norm = d_depth * d_depth + (d_row * d_row + (d_col * d_col + 4.0))
    lambert = jnp.abs(along) * lax.rsqrt(norm)
    log_t = log_t + gamma * jnp.log2(1.0 + jnp.exp(x))
    after = jnp.exp2(log_t)
    taken = passing - after
    lit = taken * lambert
    shade = shade + lit
    tinted = tinted + (taken + ratio * lit) * jnp.tanh(x)
    return log_t, after, shade, tinted


def fresh_state():
    zero = jnp.zeros((SUBLANES, LANES), jnp.float32)
    return zero, jnp.ones((SUBLANES, LANES), jnp.float32), zero, zero


def put(out, c, row, state):
    log_t, _, shade, tinted = state
    rows = pl.ds(row - SUBLANES, SUBLANES)
    lanes = pl.ds((c - 1) * LANES, LANES)
    if not isinstance(row, int):
        rows = pl.ds(pl.multiple_of(row - SUBLANES, SUBLANES), SUBLANES)
    if not isinstance(c, int):
        lanes = pl.ds(pl.multiple_of((c - 1) * LANES, LANES), LANES)
    for channel, value in enumerate((shade, tinted, log_t)):
        out[channel, rows, lanes] = value


class Bricks:
    def __init__(self, volume, cells, sems, shift, chunks, pieces):
        self.volume, self.cells, self.sems, self.pieces = volume, cells, sems, pieces
        self.chunks = chunks
        self.total = volume.shape[2] // LANES
        block = lax.rem(lax.axis_index("depth") + shift, lax.axis_size("depth"))
        self.base = block * chunks
        self.has_left = self.base > 0
        self.has_right = self.base + chunks < self.total

    def lanes(self, c):
        at = jnp.clip(self.base + (c - 1), 0, self.total - 1)
        return pl.ds(pl.multiple_of(at * LANES, LANES), LANES)

    def copy(self, c, k):
        z, depth, y, height = self.pieces[k]
        return pltpu.make_async_copy(
            self.volume.at[pl.ds(z, depth), pl.ds(y, height), self.lanes(c)],
            self.cells.at[c, pl.ds(z + 1, depth), pl.ds(y + SUBLANES, height), :],
            self.sems.at[c, k],
        )

    def clear(self, c):
        slices, rows, _ = self.volume.shape
        zero = jnp.zeros((SUBLANES, LANES), jnp.float32)

        def slice_of(z, carry):
            for r in range(rows // SUBLANES):
                self.cells[c, z + 1, pl.ds(SUBLANES * (r + 1), SUBLANES), :] = zero
            return carry

        lax.fori_loop(0, slices, slice_of, 0)

    def start(self, k, chunks):
        for c in chunks:
            if c == 0:
                pl.when(self.has_left)(lambda: self.copy(0, k).start())
            elif c == self.chunks + 1:
                pl.when(self.has_right)(lambda: self.copy(self.chunks + 1, k).start())
            else:
                self.copy(c, k).start()

    def start_all(self):
        for k in range(len(self.pieces)):
            self.start(k, (1, 0, 2))
        for c in range(3, self.chunks + 2):
            for k in range(len(self.pieces)):
                self.start(k, (c,))
        pl.when(jnp.logical_not(self.has_left))(lambda: self.clear(0))
        pl.when(jnp.logical_not(self.has_right))(lambda: self.clear(self.chunks + 1))

    def land(self, c, k):
        @pl.when(c == 1)
        def _():
            self.copy(1, k).wait()
            self.copy(2, k).wait()
            pl.when(self.has_left)(lambda: self.copy(0, k).wait())

        @pl.when(jnp.logical_and(c > 1, jnp.logical_or(c < self.chunks, self.has_right)))
        def _():
            self.copy(c + 1, k).wait()


class Edges:
    def __init__(self, bricks, sems, slab_a, slab_b, strip_a, strip_b):
        self.bricks, self.sems = bricks, sems
        self.slabs, self.strips = (slab_a, slab_b), (strip_a, strip_b)

    def slab(self, c, side, source):
        slices, rows, _ = self.bricks.volume.shape
        return pltpu.make_async_copy(
            self.slabs[source].at[0, :, self.bricks.lanes(c)],
            self.bricks.cells.at[c, side * (slices + 1), pl.ds(SUBLANES, rows), :],
            self.sems.at[c, side],
        )

    def strip(self, c, side, source):
        slices, rows, _ = self.bricks.volume.shape
        row = (SUBLANES - 1, SUBLANES + rows)[side]
        return pltpu.make_async_copy(
            self.strips[source].at[:, :, self.bricks.lanes(c)],
            self.bricks.cells.at[c, pl.ds(1, slices), pl.ds(row, 1), :],
            self.sems.at[c, 2 + side],
        )

    def start(self, chunks):
        for axis, copy in (("depth", self.slab), ("row", self.strip)):
            by_parity(
                axis,
                lambda: start(*[copy(c, side, 1 - side) for c in chunks for side in range(2)]),
                lambda: start(*[copy(c, side, side) for c in chunks for side in range(2)]),
            )

    def wait(self, c):
        for side in range(2):
            self.slab(c, side, 0).wait()
            self.strip(c, side, 0).wait()


def march(cells, c, rows, begin, step, trips, coef, ends, arrive):
    def at(z):
        return [cells[c, z, pl.ds(row, SUBLANES), :] for row in rows]

    def trip(k, carry):
        arrive(k)
        states, belows, centers = carry
        for i in range(step):
            z = begin + 1 + k * step + i
            aboves = at(z + 1)
            states = [
                cell(cells, c, z, *tile, coef, ends)
                for tile in zip(rows, centers, belows, aboves, states)
            ]
            belows, centers = centers, aboves
        return states, belows, centers

    carry = ([fresh_state()] * len(rows), at(begin), at(begin + 1))
    if trips == 1:
        return trip(0, carry)[0]
    return lax.fori_loop(0, trips, trip, carry)[0]


def full_kernel(shift, tiles, pieces, total_slices, transfer, volume, *refs):
    *halo, out, cells, sems, edge_sems = refs
    slices, rows, _ = volume.shape
    chunks = out.shape[2] // LANES
    trips = len(pieces)
    groups = rows // SUBLANES // tiles
    bricks = Bricks(volume, cells, sems, shift, chunks, pieces)
    edges = Edges(bricks, edge_sems, *halo)
    bricks.start_all()
    edges.start(range(1, chunks + 1))
    coef = coefficients(transfer, total_slices)
    ends = tile_constants()

    def group(index, carry):
        c = index // groups + 1
        row = pl.multiple_of((index % groups * tiles + 1) * SUBLANES, SUBLANES)
        fresh = index % groups == 0

        @pl.when(fresh)
        def _():
            edges.wait(c)
            bricks.land(c, 0)

        def arrive(k):
            for part in range(1, trips):
                pl.when(jnp.logical_and(fresh, k == part))(lambda part=part: bricks.land(c, part))

        at_rows = [row + SUBLANES * t for t in range(tiles)]
        states = march(cells, c, at_rows, 0, slices // trips, trips, coef, ends, arrive)
        for at_row, state in zip(at_rows, states):
            put(out, c, at_row, state)
        return carry

    lax.fori_loop(0, chunks * groups, group, 0)


def inner_kernel(shift, pieces, total_slices, transfer, volume, out, cells, sems):
    slices, rows, _ = volume.shape
    chunks = out.shape[2] // LANES
    trips = len(pieces)
    bricks = Bricks(volume, cells, sems, shift, chunks, pieces)
    bricks.start_all()
    coef = coefficients(transfer, total_slices)
    ends = tile_constants()
    at_rows = [SUBLANES * (t + 2) for t in range(rows // SUBLANES - 2)]

    def group(index, carry):
        c = index + 1
        bricks.land(c, 0)

        def arrive(k):
            for part in range(1, trips):
                pl.when(k == part)(lambda part=part: bricks.land(c, part))

        states = march(
            cells, c, at_rows, 1, (slices - 2) // trips, trips, coef, ends, arrive
        )
        for at_row, state in zip(at_rows, states):
            put(out, c, at_row, state)
        return carry

    lax.fori_loop(0, chunks, group, 0)


def rest_kernel(shift, pieces, total_slices, transfer, volume, *refs):
    *halo, inner, out, cells, sems, edge_sems = refs
    slices, rows, _ = volume.shape
    chunks = out.shape[2] // LANES
    bricks = Bricks(volume, cells, sems, shift, chunks, pieces)
    edges = Edges(bricks, edge_sems, *halo)
    bricks.start_all()
    edges.start(range(1, chunks + 1))
    coef = coefficients(transfer, total_slices)
    ends = tile_constants()

    def group(index, carry):
        c = index + 1
        edges.wait(c)
        for k in range(len(pieces)):
            bricks.land(c, k)
        outer = [SUBLANES, rows]
        states = march(cells, c, outer, 0, slices, 1, coef, ends, lambda k: None)
        for at_row, state in zip(outer, states):
            put(out, c, at_row, state)
        lanes = pl.ds(pl.multiple_of((c - 1) * LANES, LANES), LANES)
        for t in range(1, rows // SUBLANES - 1):
            row = SUBLANES * (t + 1)
            here = pl.ds(row, SUBLANES)
            sides = []
            for z in (1, slices):
                below, x, above = [cells[c, z + i, here, :] for i in (-1, 0, 1)]
                sides.append(cell(cells, c, z, row, x, below, above, fresh_state(), coef, ends))
            (log_a, pass_a, shade_a, tint_a), (log_b, _, shade_b, tint_b) = sides
            shade, tint, log_t = [inner[i, pl.ds(row - SUBLANES, SUBLANES), lanes] for i in range(3)]
            passing = jnp.exp2(log_t)
            shade = shade_a + pass_a * (shade + passing * shade_b)
            tint = tint_a + pass_a * (tint + passing * tint_b)
            put(out, c, row, (log_a + log_t + log_b, None, shade, tint))
        return carry

    lax.fori_loop(0, chunks, group, 0)


def render(kernel, pieces, transfer, volume, extra, width, halo):
    slices, rows, _ = volume.shape
    chunks = width // LANES
    scratch = [
        pltpu.VMEM((chunks + 2, slices + 2, rows + 2 * SUBLANES, LANES), jnp.float32),
        pltpu.SemaphoreType.DMA((chunks + 2, len(pieces))),
    ]
    if halo:
        scratch.append(pltpu.SemaphoreType.DMA((chunks + 1, 4)))
    return pl.pallas_call(
        kernel,
        in_specs=[SMEM, ANY] + [ANY] * min(4, len(extra)) + [VMEM] * (len(extra) - 4),
        out_specs=VMEM,
        out_shape=jax.ShapeDtypeStruct((3, rows, width), jnp.float32),
        scratch_shapes=scratch,
        compiler_params=pltpu.CompilerParams(vmem_limit_bytes=32 << 20),
    )(transfer, volume, *extra)


def merge_kernel(shifts, transfer, *refs):
    *parts, out = refs
    count = len(parts)
    mine = lax.axis_index("depth")
    rows, width = out.shape[1:]
    sources = [lax.rem(mine - shift + count, count) for shift in shifts]
    nearer = [
        [jnp.where(sources[j] < sources[i], 1.0, 0.0) for j in range(count)] for i in range(count)
    ]
    ambient = 0.5 * jnp.full((SUBLANES, LANES), transfer[7], jnp.float32)
    spread = (1.0 - ambient) / 3.0

    def band(r, carry):
        here = pl.ds(pl.multiple_of(r * SUBLANES, SUBLANES), SUBLANES)
        for x in range(width // LANES):
            at = pl.ds(x * LANES, LANES)
            shade = tinted = log_t = jnp.zeros((SUBLANES, LANES), jnp.float32)
            logs = [part[2, here, at] for part in parts]
            for i, part in enumerate(parts):
                ahead = sum(logs[j] * nearer[i][j] for j in range(count) if j != i)
                passing = jnp.exp2(ahead)
                shade = shade + passing * part[0, here, at]
                tinted = tinted + passing * part[1, here, at]
                log_t = log_t + logs[i]
            half = jnp.tanh(log_t * (-0.5 * LN2))
            opacity = (half + half) / (1.0 + half)
            full = ambient * opacity + spread * shade
            mixed = 0.5 * (full + ambient * tinted)
            for color in range(3):
                out[color, here, at] = transfer[color] * full + transfer[3 + color] * mixed
            out[3, here, at] = opacity
        return carry

    lax.fori_loop(0, rows // SUBLANES, band, 0)


def merge(parts, shifts, transfer):
    _, rows, width = parts[0].shape
    return pl.pallas_call(
        functools.partial(merge_kernel, shifts),
        in_specs=[SMEM] + [VMEM] * len(parts),
        out_specs=VMEM,
        out_shape=jax.ShapeDtypeStruct((4, rows, width), jnp.float32),
        compiler_params=pltpu.CompilerParams(vmem_limit_bytes=16 << 20),
        name="merge",
    )(transfer, *parts)


def on_device(volume, transfer):
    slices, rows, columns = volume.shape
    groups = lax.axis_size("depth")
    total_slices = slices * groups
    width = columns // groups
    slab_a, slab_b, strip_a, strip_b = cut(volume)
    edges = (
        swap(slab_a, "depth", 0),
        swap(slab_b, "depth", 1),
        swap(strip_a, "row", 0),
        swap(strip_b, "row", 1),
    )
    half = slices // 2
    halves = [(0, half + 1, 0, rows), (half + 1, slices - half - 1, 0, rows)]
    ring = [
        (0, slices, 0, 2 * SUBLANES),
        (0, slices, rows - 2 * SUBLANES, 2 * SUBLANES),
        (0, 2, 2 * SUBLANES, rows - 4 * SUBLANES),
        (slices - 2, 2, 2 * SUBLANES, rows - 4 * SUBLANES),
    ]
    shifts = order_of_shifts(groups)
    parts = []
    for stage, shift in enumerate(shifts):
        if stage == 0:
            kernel = functools.partial(inner_kernel, shift, halves, total_slices)
            inner = render(kernel, halves, transfer, volume, (), width, False)
            kernel = functools.partial(rest_kernel, shift, ring, total_slices)
            part = render(kernel, ring, transfer, volume, edges + (inner,), width, True)
        else:
            kernel = functools.partial(full_kernel, shift, 8, halves, total_slices)
            part = render(kernel, halves, transfer, volume, edges, width, True)
        if shift:
            pairs = [(i, (i + shift) % groups) for i in range(groups)]
            part = lax.ppermute(part, "depth", pairs)
        parts.append(part)
    return merge(parts, shifts, transfer)


def order_of_shifts(groups):
    return sorted(range(1, groups), key=lambda s: -min(s, groups - s)) + [0]


def solution(mesh):
    in_specs = (P("depth", "row", None), P())
    out_specs = P(None, "row", "depth")

    return jax.shard_map(
        on_device, mesh=mesh, in_specs=in_specs, out_specs=out_specs, check_vma=False
    )
```

profile of v0, /device:TPU:0, one launch (start us, length us, event | category | flops | bytes accessed | tf_op | source)
XLA Modules:
  0.0 72.6 jit_solution(3341294239727294258)
XLA Ops:
  0.0 0.0 copy-start
  0.0 2.7 %cut.1 = (f32[1,64,2048]{2,1,0:T(8,128)}, f32[1,64,2048]{2,1,0:T(8,128)}, f32[48,1,2048]{2,1,0:T(1,128)}, f32[48,1,2048]{2,1,0:T(1,128)}) custom-call(f32[48,64,2048]{2,1,0:T(8,128)} %volume.11), custom_call_target="tpu_custom_call" | custom-call | tf_op jit(solution)/shard_map/cut/pallas_call | solution.py:61
  2.7 3.1 %collective-permute-start = (f32[1,64,2048]{2,1,0:T(8,128)}, f32[1,64,2048]{2,1,0:T(8,128)S(1)}, u32[]{:S(2)}, u32[]{:S(2)}) collective-permute-start(f32[1,64,2048]{2,1,0:T(8,128)} %get-tuple-element.9), channel_id=1, source_target_pairs={{0,8},{8,0},{16,24},{24,16},{1,9},{9,1},{17,25},{25,17},{2,10},{10... | collective-permute-start | bytes 1572872 | tf_op jit(solution)/shard_map/ppermute | solution.py:75
  5.8 0.7 collective-permute-start.1
  6.5 0.1 collective-permute-start.2
  6.6 0.7 collective-permute-start.3
  7.3 0.0 copy-done
  7.3 7.7 %shard_map.28.refs_4_ = f32[3,64,512]{2,1,0:T(8,128)S(1)} custom-call(f32[8]{0:T(128)S(1)} %copy-done, f32[48,64,2048]{2,1,0:T(8,128)} %volume.11), custom_call_target="tpu_custom_call" | custom-call | tf_op jit(solution)/shard_map/pallas_call | solution.py:365
  15.0 0.0 collective-permute-done.2.refs_2_
  15.0 0.0 collective-permute-done.3.refs_3_
  15.0 3.0 %collective-permute-done.refs_0_ = f32[1,64,2048]{2,1,0:T(8,128)S(1)} collective-permute-done((f32[1,64,2048]{2,1,0:T(8,128)}, f32[1,64,2048]{2,1,0:T(8,128)S(1)}, u32[]{:S(2)}, u32[]{:S(2)}) %collective-permute-start) | collective-permute-done | bytes 524320 | tf_op jit(solution)/shard_map/ppermute | solution.py:75
  18.0 0.0 collective-permute-done.1.refs_1_
  18.0 9.5 %shard_map.30 = f32[3,64,512]{2,1,0:T(8,128)S(1)} custom-call(f32[8]{0:T(128)S(1)} %copy-done, f32[48,64,2048]{2,1,0:T(8,128)} %volume.11, f32[1,64,2048]{2,1,0:T(8,128)S(1)} %collective-permute-done.refs_0_, f32[1,64,2048]{2,1,0:T(8,128)S(1)} %collective-permute-done.1.refs_1_, f32[48,1,2048]{2,1,0:T(1,128)S(1)} %collective-permute-done.2.refs_2_, ...), custom_call_target="tpu_custom_call" | custom-call | tf_op jit(solution)/shard_map/pallas_call | solution.py:365
  27.5 4.8 %collective-permute-start.5 = (f32[3,64,512]{2,1,0:T(8,128)S(1)}, f32[3,64,512]{2,1,0:T(8,128)S(1)}, u32[]{:S(2)}, u32[]{:S(2)}) collective-permute-start(f32[3,64,512]{2,1,0:T(8,128)S(1)} %shard_map.30), channel_id=1, source_target_pairs={{0,8},{8,16},{16,24},{24,0},{1,9},{9,17},{17,25},{25,1},{2,10},{10... | collective-permute-start | bytes 1179656 | tf_op jit(solution)/shard_map/ppermute | solution.py:456
  32.3 9.5 %shard_map.31 = f32[3,64,512]{2,1,0:T(8,128)S(1)} custom-call(f32[8]{0:T(128)S(1)} %copy-done, f32[48,64,2048]{2,1,0:T(8,128)} %volume.11, f32[1,64,2048]{2,1,0:T(8,128)S(1)} %collective-permute-done.refs_0_, f32[1,64,2048]{2,1,0:T(8,128)S(1)} %collective-permute-done.1.refs_1_, f32[48,1,2048]{2,1,0:T(1,128)S(1)} %collective-permute-done.2.refs_2_, ...), custom_call_target="tpu_custom_call" | custom-call | tf_op jit(solution)/shard_map/pallas_call | solution.py:365
  41.8 0.1 collective-permute-start.6
  41.8 4.6 %shard_map.29 = f32[3,64,512]{2,1,0:T(8,128)S(1)} custom-call(f32[8]{0:T(128)S(1)} %copy-done, f32[48,64,2048]{2,1,0:T(8,128)} %volume.11, f32[1,64,2048]{2,1,0:T(8,128)S(1)} %collective-permute-done.refs_0_, f32[1,64,2048]{2,1,0:T(8,128)S(1)} %collective-permute-done.1.refs_1_, f32[48,1,2048]{2,1,0:T(1,128)S(1)} %collective-permute-done.2.refs_2_, ...), custom_call_target="tpu_custom_call" | custom-call | tf_op jit(solution)/shard_map/pallas_call | solution.py:365
  46.5 2.7 %collective-permute-start.4 = (f32[3,64,512]{2,1,0:T(8,128)S(1)}, f32[3,64,512]{2,1,0:T(8,128)S(1)}, u32[]{:S(2)}, u32[]{:S(2)}) collective-permute-start(f32[3,64,512]{2,1,0:T(8,128)S(1)} %shard_map.29), channel_id=1, source_target_pairs={{0,16},{8,24},{16,0},{24,8},{1,17},{9,25},{17,1},{25,9},{2,18},{10... | collective-permute-start | bytes 1179656 | tf_op jit(solution)/shard_map/ppermute | solution.py:456
  49.2 9.2 %shard_map.32.refs_3_ = f32[3,64,512]{2,1,0:T(8,128)S(1)} custom-call(f32[8]{0:T(128)S(1)} %copy-done, f32[48,64,2048]{2,1,0:T(8,128)} %volume.11, f32[1,64,2048]{2,1,0:T(8,128)S(1)} %collective-permute-done.refs_0_, f32[1,64,2048]{2,1,0:T(8,128)S(1)} %collective-permute-done.1.refs_1_, f32[48,1,2048]{2,1,0:T(1,128)S(1)} %collective-permute-done.2.refs_2_, ...), custom_call_target="tpu_custom_call" | custom-call | tf_op jit(solution)/shard_map/pallas_call | solution.py:365
  58.4 0.0 collective-permute-done.5.refs_1_
  58.4 0.0 collective-permute-done.6.refs_2_
  58.4 12.4 %collective-permute-done.4.refs_0_ = f32[3,64,512]{2,1,0:T(8,128)S(1)} collective-permute-done((f32[3,64,512]{2,1,0:T(8,128)S(1)}, f32[3,64,512]{2,1,0:T(8,128)S(1)}, u32[]{:S(2)}, u32[]{:S(2)}) %collective-permute-start.4) | collective-permute-done | bytes 393248 | tf_op jit(solution)/shard_map/ppermute | solution.py:456
  70.8 1.8 %merge.1 = f32[4,64,512]{2,1,0:T(8,128)} custom-call(f32[8]{0:T(128)S(1)} %copy-done, f32[3,64,512]{2,1,0:T(8,128)S(1)} %collective-permute-done.4.refs_0_, f32[3,64,512]{2,1,0:T(8,128)S(1)} %collective-permute-done.5.refs_1_, f32[3,64,512]{2,1,0:T(8,128)S(1)} %collective-permute-done.6.refs_2_, f32[3,64,512]{2,1,0:T(8,128)S(1)} %shard_map.32.refs_3_), custom_call_target="tpu_custom_call" | custom-call | tf_op jit(solution)/shard_map/merge/pallas_call | solution.py:413
Async XLA Ops:
  0.0 7.3 %copy-start = (f32[8]{0:T(128)S(1)}, f32[8]{0:T(128)}, u32[]{:S(2)}) copy-start(f32[8]{0:T(128)} %transfer.11) | copy-start | bytes 100
  2.7 15.3 %collective-permute-start = (f32[1,64,2048]{2,1,0:T(8,128)}, f32[1,64,2048]{2,1,0:T(8,128)S(1)}, u32[]{:S(2)}, u32[]{:S(2)}) collective-permute-start(f32[1,64,2048]{2,1,0:T(8,128)} %get-tuple-element.9), channel_id=1, source_target_pairs={{0,8},{8,0},{16,24},{24,16},{1,9},{9,1},{17,25},{25,17},{2,10},{10... | collective-permute-start | bytes 1572872 | tf_op jit(solution)/shard_map/ppermute | solution.py:75
  5.8 12.1 %collective-permute-start.1 = (f32[1,64,2048]{2,1,0:T(8,128)}, f32[1,64,2048]{2,1,0:T(8,128)S(1)}, u32[]{:S(2)}, u32[]{:S(2)}) collective-permute-start(f32[1,64,2048]{2,1,0:T(8,128)} %get-tuple-element.10), channel_id=1, source_target_pairs={{8,16},{16,8},{9,17},{17,9},{10,18},{18,10},{11,19},{19,11},{12,20... | collective-permute-start | bytes 1572872 | tf_op jit(solution)/shard_map/ppermute | solution.py:75
  6.5 8.5 %collective-permute-start.2 = (f32[48,1,2048]{2,1,0:T(1,128)}, f32[48,1,2048]{2,1,0:T(1,128)S(1)}, u32[]{:S(2)}, u32[]{:S(2)}) collective-permute-start(f32[48,1,2048]{2,1,0:T(1,128)} %get-tuple-element.11), channel_id=1, source_target_pairs={{0,1},{1,0},{2,3},{3,2},{4,5},{5,4},{6,7},{7,6},{8,9},{9,8},{10,11... | collective-permute-start | bytes 1179656 | tf_op jit(solution)/shard_map/ppermute | solution.py:75
  6.6 8.4 %collective-permute-start.3 = (f32[48,1,2048]{2,1,0:T(1,128)}, f32[48,1,2048]{2,1,0:T(1,128)S(1)}, u32[]{:S(2)}, u32[]{:S(2)}) collective-permute-start(f32[48,1,2048]{2,1,0:T(1,128)} %get-tuple-element.12), channel_id=1, source_target_pairs={{1,2},{2,1},{3,4},{4,3},{5,6},{6,5},{9,10},{10,9},{11,12},{12,11},... | collective-permute-start | bytes 1179656 | tf_op jit(solution)/shard_map/ppermute | solution.py:75
  27.5 30.9 %collective-permute-start.5 = (f32[3,64,512]{2,1,0:T(8,128)S(1)}, f32[3,64,512]{2,1,0:T(8,128)S(1)}, u32[]{:S(2)}, u32[]{:S(2)}) collective-permute-start(f32[3,64,512]{2,1,0:T(8,128)S(1)} %shard_map.30), channel_id=1, source_target_pairs={{0,8},{8,16},{16,24},{24,0},{1,9},{9,17},{17,25},{25,1},{2,10},{10... | collective-permute-start | bytes 1179656 | tf_op jit(solution)/shard_map/ppermute | solution.py:456
  41.8 16.7 %collective-permute-start.6 = (f32[3,64,512]{2,1,0:T(8,128)S(1)}, f32[3,64,512]{2,1,0:T(8,128)S(1)}, u32[]{:S(2)}, u32[]{:S(2)}) collective-permute-start(f32[3,64,512]{2,1,0:T(8,128)S(1)} %shard_map.31), channel_id=1, source_target_pairs={{0,24},{8,0},{16,8},{24,16},{1,25},{9,1},{17,9},{25,17},{2,26},{10... | collective-permute-start | bytes 1179656 | tf_op jit(solution)/shard_map/ppermute | solution.py:456
  46.5 24.4 %collective-permute-start.4 = (f32[3,64,512]{2,1,0:T(8,128)S(1)}, f32[3,64,512]{2,1,0:T(8,128)S(1)}, u32[]{:S(2)}, u32[]{:S(2)}) collective-permute-start(f32[3,64,512]{2,1,0:T(8,128)S(1)} %shard_map.29), channel_id=1, source_target_pairs={{0,16},{8,24},{16,0},{24,8},{1,17},{9,25},{17,1},{25,9},{2,18},{10... | collective-permute-start | bytes 1179656 | tf_op jit(solution)/shard_map/ppermute | solution.py:456
where the time goes:
time: 72.7 us; the launch traced here: 72.6 us
  Pallas kernels  44.9 us (62%)
  waiting for transfers between devices  15.4 us (21%)
  starting transfers between devices  12.2 us (17%)
    pallas_call x5, Pallas kernels, render(): pl.pallas_call(kernel, in_specs=[SMEM, ANY] + [ANY] * min(4, len(extra))...  40.4 us
    ppermute x3, waiting for transfers between devices, on_device(): part = lax.ppermute(part, 'depth', pairs)  12.4 us
    ppermute x3, starting transfers between devices, on_device(): part = lax.ppermute(part, 'depth', pairs)  7.6 us
    ppermute x4, starting transfers between devices, swap(): return lax.ppermute(value, axis, pairs)  4.56 us
    ppermute x4, waiting for transfers between devices, swap(): return lax.ppermute(value, axis, pairs)  2.98 us
    pallas_call x1, Pallas kernels, cut(): pl.pallas_call(cut_kernel, in_specs=[ANY], out_specs=[VMEM] * 4, out_shap...  2.72 us
    pallas_call x1, Pallas kernels, merge(): pl.pallas_call(functools.partial(merge_kernel, shifts), in_specs=[SMEM] +...  1.75 us
  transfers between devices with their start and end apart: 7, of which 2 were waited for; matrix products, arithmetic and copies ran while one was open for 0% of the time, Pallas kernels for 43%

commit v1 on v0

--- a/solution.py
+++ b/solution.py
@@ -314,13 +314,12 @@
     lax.fori_loop(0, chunks, group, 0)
 
 
-def rest_kernel(shift, pieces, total_slices, transfer, volume, *refs):
-    *halo, inner, out, cells, sems, edge_sems = refs
+def rest_kernel(shift, total_slices, transfer, volume, *refs):
+    *halo, inner, _, out, cells, edge_sems = refs
     slices, rows, _ = volume.shape
     chunks = out.shape[2] // LANES
-    bricks = Bricks(volume, cells, sems, shift, chunks, pieces)
+    bricks = Bricks(volume, cells, None, shift, chunks, ())
     edges = Edges(bricks, edge_sems, *halo)
-    bricks.start_all()
     edges.start(range(1, chunks + 1))
     coef = coefficients(transfer, total_slices)
     ends = tile_constants()
@@ -328,8 +327,6 @@
     def group(index, carry):
         c = index + 1
         edges.wait(c)
-        for k in range(len(pieces)):
-            bricks.land(c, k)
         outer = [SUBLANES, rows]
         states = march(cells, c, outer, 0, slices, 1, coef, ends, lambda k: None)
         for at_row, state in zip(outer, states):
@@ -351,6 +348,41 @@
         return carry
 
     lax.fori_loop(0, chunks, group, 0)
+
+
+def cells_shape(volume, width):
+    slices, rows, _ = volume.shape
+    return (width // LANES + 2, slices + 2, rows + 2 * SUBLANES, LANES)
+
+
+def render_inner(kernel, pieces, transfer, volume, width):
+    shape = cells_shape(volume, width)
+    return pl.pallas_call(
+        kernel,
+        in_specs=[SMEM, ANY],
+        out_specs=[VMEM] * 2,
+        out_shape=[
+            jax.ShapeDtypeStruct((3, volume.shape[1], width), jnp.float32),
+            jax.ShapeDtypeStruct(shape, jnp.float32),
+        ],
+        scratch_shapes=[pltpu.SemaphoreType.DMA((shape[0], len(pieces)))],
+        compiler_params=pltpu.CompilerParams(vmem_limit_bytes=32 << 20),
+        name="inner",
+    )(transfer, volume)
+
+
+def render_rest(kernel, transfer, volume, halo, inner, cells):
+    out = jax.ShapeDtypeStruct(inner.shape, jnp.float32)
+    return pl.pallas_call(
+        kernel,
+        in_specs=[SMEM, ANY] + [ANY] * 4 + [VMEM] * 2,
+        out_specs=[VMEM] * 2,
+        out_shape=[out, jax.ShapeDtypeStruct(cells.shape, jnp.float32)],
+        input_output_aliases={7: 1},
+        scratch_shapes=[pltpu.SemaphoreType.DMA((cells.shape[0] - 1, 4))],
+        compiler_params=pltpu.CompilerParams(vmem_limit_bytes=32 << 20),
+        name="rest",
+    )(transfer, volume, *halo, inner, cells)[0]
 
 
 def render(kernel, pieces, transfer, volume, extra, width, halo):
@@ -434,20 +466,14 @@
     )
     half = slices // 2
     halves = [(0, half + 1, 0, rows), (half + 1, slices - half - 1, 0, rows)]
-    ring = [
-        (0, slices, 0, 2 * SUBLANES),
-        (0, slices, rows - 2 * SUBLANES, 2 * SUBLANES),
-        (0, 2, 2 * SUBLANES, rows - 4 * SUBLANES),
-        (slices - 2, 2, 2 * SUBLANES, rows - 4 * SUBLANES),
-    ]
     shifts = order_of_shifts(groups)
     parts = []
     for stage, shift in enumerate(shifts):
         if stage == 0:
             kernel = functools.partial(inner_kernel, shift, halves, total_slices)
-            inner = render(kernel, halves, transfer, volume, (), width, False)
-            kernel = functools.partial(rest_kernel, shift, ring, total_slices)
-            part = render(kernel, ring, transfer, volume, edges + (inner,), width, True)
+            inner, cells = render_inner(kernel, halves, transfer, volume, width)
+            kernel = functools.partial(rest_kernel, shift, total_slices)
+            part = render_rest(kernel, transfer, volume, edges, inner, cells)
         else:
             kernel = functools.partial(full_kernel, shift, 8, halves, total_slices)
             part = render(kernel, halves, transfer, volume, edges, width, True)

time: 72.7 us -> 63.7 us (0.88)
  waiting for transfers between devices: 15.4 us -> 5.56 us
  starting transfers between devices: 12.2 us -> 14.5 us
  Pallas kernels: 44.9 us -> 43.4 us
    pallas_call x5 -> x3, Pallas kernels: 40.4 us -> 28.2 us  [render(): pl.pallas_call(kernel, in_specs=[SMEM, ANY] + [ANY] * min(4, len(extra))...]
    pallas_call x0 -> x2, Pallas kernels: none -> 10.8 us  [the longest x1 7.74 us: render_inner(): pl.pallas_call(kernel, in_specs=[SMEM, ANY], out_specs=[VMEM] * 2, out_sh...]
    ppermute x3, waiting for transfers between devices: 12.4 us -> 2.66 us  [on_device(): part = lax.ppermute(part, 'depth', pairs)]
    ppermute x3, starting transfers between devices: 7.6 us -> 9.91 us  [on_device(): part = lax.ppermute(part, 'depth', pairs)]
  transfers between devices with their start and end apart: 7 -> 7, of which waited for: 2 -> 2; matrix products, arithmetic and copies ran while one was open for 0% -> 0% of each run, Pallas kernels for 43% -> 56%
where the time goes in v1:
time: 63.7 us; the launch traced here: 63.6 us
  Pallas kernels  43.4 us (68%)
  starting transfers between devices  14.5 us (23%)
  waiting for transfers between devices  5.56 us (9%)
    pallas_call x3, Pallas kernels, render(): pl.pallas_call(kernel, in_specs=[SMEM, ANY] + [ANY] * min(4, len(extra))...  28.2 us
    ppermute x3, starting transfers between devices, on_device(): part = lax.ppermute(part, 'depth', pairs)  9.91 us
    pallas_call x1, Pallas kernels, render_inner(): pl.pallas_call(kernel, in_specs=[SMEM, ANY], out_specs=[VMEM] * 2, out_sh...  7.74 us
    ppermute x4, starting transfers between devices, swap(): return lax.ppermute(value, axis, pairs)  4.56 us
    pallas_call x1, Pallas kernels, render_rest(): pl.pallas_call(kernel, in_specs=[SMEM, ANY] + [ANY] * 4 + [VMEM] * 2, out...  3.02 us
    ppermute x4, waiting for transfers between devices, swap(): return lax.ppermute(value, axis, pairs)  2.9 us
    pallas_call x1, Pallas kernels, cut(): pl.pallas_call(cut_kernel, in_specs=[ANY], out_specs=[VMEM] * 4, out_shap...  2.72 us
    ppermute x3, waiting for transfers between devices, on_device(): part = lax.ppermute(part, 'depth', pairs)  2.66 us
  transfers between devices with their start and end apart: 7, of which 2 were waited for; matrix products, arithmetic and copies ran while one was open for 0% of the time, Pallas kernels for 56%

profile of v1, /device:TPU:0, one launch (start us, length us, event | category | flops | bytes accessed | tf_op | source)
XLA Modules:
  0.0 63.6 jit_solution(5125067978592624338)
XLA Ops:
  0.0 0.0 copy-start
  0.0 2.7 %cut.1 = (f32[1,64,2048]{2,1,0:T(8,128)}, f32[1,64,2048]{2,1,0:T(8,128)}, f32[48,1,2048]{2,1,0:T(1,128)}, f32[48,1,2048]{2,1,0:T(1,128)}) custom-call(f32[48,64,2048]{2,1,0:T(8,128)} %volume.11), custom_call_target="tpu_custom_call" | custom-call | tf_op jit(solution)/shard_map/cut/pallas_call | solution.py:61
  2.7 3.1 %collective-permute-start = (f32[1,64,2048]{2,1,0:T(8,128)}, f32[1,64,2048]{2,1,0:T(8,128)S(1)}, u32[]{:S(2)}, u32[]{:S(2)}) collective-permute-start(f32[1,64,2048]{2,1,0:T(8,128)} %get-tuple-element.12), channel_id=1, source_target_pairs={{0,8},{8,0},{16,24},{24,16},{1,9},{9,1},{17,25},{25,17},{2,10},{10... | collective-permute-start | bytes 1572872 | tf_op jit(solution)/shard_map/ppermute | solution.py:75
  5.8 0.7 %collective-permute-start.1 = (f32[1,64,2048]{2,1,0:T(8,128)}, f32[1,64,2048]{2,1,0:T(8,128)S(1)}, u32[]{:S(2)}, u32[]{:S(2)}) collective-permute-start(f32[1,64,2048]{2,1,0:T(8,128)} %get-tuple-element.13), channel_id=1, source_target_pairs={{8,16},{16,8},{9,17},{17,9},{10,18},{18,10},{11,19},{19,11},{12,20... | collective-permute-start | bytes 1572872 | tf_op jit(solution)/shard_map/ppermute | solution.py:75
  6.5 0.1 collective-permute-start.2
  6.6 0.7 %collective-permute-start.3 = (f32[48,1,2048]{2,1,0:T(1,128)}, f32[48,1,2048]{2,1,0:T(1,128)S(1)}, u32[]{:S(2)}, u32[]{:S(2)}) collective-permute-start(f32[48,1,2048]{2,1,0:T(1,128)} %get-tuple-element.15), channel_id=1, source_target_pairs={{1,2},{2,1},{3,4},{4,3},{5,6},{6,5},{9,10},{10,9},{11,12},{12,11},... | collective-permute-start | bytes 1179656 | tf_op jit(solution)/shard_map/ppermute | solution.py:75
  7.3 0.0 copy-done
  7.3 7.7 %inner.1 = (f32[3,64,512]{2,1,0:T(8,128)S(1)}, f32[6,50,80,128]{3,2,1,0:T(8,128)S(1)}) custom-call(f32[8]{0:T(128)S(1)} %copy-done, f32[48,64,2048]{2,1,0:T(8,128)} %volume.11), custom_call_target="tpu_custom_call" | custom-call | tf_op jit(solution)/shard_map/inner/pallas_call | solution.py:360
  15.1 0.0 collective-permute-done.2.refs_2_
  15.1 0.0 collective-permute-done.3.refs_3_
  15.1 2.9 %collective-permute-done.refs_0_ = f32[1,64,2048]{2,1,0:T(8,128)S(1)} collective-permute-done((f32[1,64,2048]{2,1,0:T(8,128)}, f32[1,64,2048]{2,1,0:T(8,128)S(1)}, u32[]{:S(2)}, u32[]{:S(2)}) %collective-permute-start) | collective-permute-done | bytes 524320 | tf_op jit(solution)/shard_map/ppermute | solution.py:75
  18.0 0.0 collective-permute-done.1.refs_1_
  18.0 3.0 %rest.1 = (f32[3,64,512]{2,1,0:T(8,128)S(1)}, f32[6,50,80,128]{3,2,1,0:T(8,128)S(1)}) custom-call(f32[8]{0:T(128)S(1)} %copy-done, f32[48,64,2048]{2,1,0:T(8,128)} %volume.11, f32[1,64,2048]{2,1,0:T(8,128)S(1)} %collective-permute-done.refs_0_, f32[1,64,2048]{2,1,0:T(8,128)S(1)} %collective-permute-done.1.refs_1_, ...), custom_call_target="tpu_custom_call", output_to_operand_aliasing={{1}: (7, {})} | custom-call | tf_op jit(solution)/shard_map/rest/pallas_call | solution.py:376
  21.0 6.0 %collective-permute-start.4 = (f32[3,64,512]{2,1,0:T(8,128)S(1)}, f32[3,64,512]{2,1,0:T(8,128)S(1)}, u32[]{:S(2)}, u32[]{:S(2)}) collective-permute-start(f32[3,64,512]{2,1,0:T(8,128)S(1)} %get-tuple-element.18), channel_id=1, source_target_pairs={{0,16},{8,24},{16,0},{24,8},{1,17},{9,25},{17,1},{25,9},{2,18},{10... | collective-permute-start | bytes 1179656 | tf_op jit(solution)/shard_map/ppermute | solution.py:482
  27.0 9.5 %shard_map.28 = f32[3,64,512]{2,1,0:T(8,128)S(1)} custom-call(f32[8]{0:T(128)S(1)} %copy-done, f32[48,64,2048]{2,1,0:T(8,128)} %volume.11, f32[1,64,2048]{2,1,0:T(8,128)S(1)} %collective-permute-done.refs_0_, f32[1,64,2048]{2,1,0:T(8,128)S(1)} %collective-permute-done.1.refs_1_, f32[48,1,2048]{2,1,0:T(1,128)S(1)} %collective-permute-done.2.refs_2_, ...), custom_call_target="tpu_custom_call" | custom-call | tf_op jit(solution)/shard_map/pallas_call | solution.py:397
  36.5 0.1 collective-permute-start.5
  36.6 9.5 %shard_map.29 = f32[3,64,512]{2,1,0:T(8,128)S(1)} custom-call(f32[8]{0:T(128)S(1)} %copy-done, f32[48,64,2048]{2,1,0:T(8,128)} %volume.11, f32[1,64,2048]{2,1,0:T(8,128)S(1)} %collective-permute-done.refs_0_, f32[1,64,2048]{2,1,0:T(8,128)S(1)} %collective-permute-done.1.refs_1_, f32[48,1,2048]{2,1,0:T(1,128)S(1)} %collective-permute-done.2.refs_2_, ...), custom_call_target="tpu_custom_call" | custom-call | tf_op jit(solution)/shard_map/pallas_call | solution.py:397
  46.0 3.9 %collective-permute-start.6 = (f32[3,64,512]{2,1,0:T(8,128)S(1)}, f32[3,64,512]{2,1,0:T(8,128)S(1)}, u32[]{:S(2)}, u32[]{:S(2)}) collective-permute-start(f32[3,64,512]{2,1,0:T(8,128)S(1)} %shard_map.29), channel_id=1, source_target_pairs={{0,24},{8,0},{16,8},{24,16},{1,25},{9,1},{17,9},{25,17},{2,26},{10... | collective-permute-start | bytes 1179656 | tf_op jit(solution)/shard_map/ppermute | solution.py:482
  49.9 9.2 %shard_map.30.refs_3_ = f32[3,64,512]{2,1,0:T(8,128)S(1)} custom-call(f32[8]{0:T(128)S(1)} %copy-done, f32[48,64,2048]{2,1,0:T(8,128)} %volume.11, f32[1,64,2048]{2,1,0:T(8,128)S(1)} %collective-permute-done.refs_0_, f32[1,64,2048]{2,1,0:T(8,128)S(1)} %collective-permute-done.1.refs_1_, f32[48,1,2048]{2,1,0:T(1,128)S(1)} %collective-permute-done.2.refs_2_, ...), custom_call_target="tpu_custom_call" | custom-call | tf_op jit(solution)/shard_map/pallas_call | solution.py:397
  59.1 0.0 collective-permute-done.4.refs_0_
  59.1 0.0 collective-permute-done.5.refs_1_
  59.1 2.7 %collective-permute-done.6.refs_2_ = f32[3,64,512]{2,1,0:T(8,128)S(1)} collective-permute-done((f32[3,64,512]{2,1,0:T(8,128)S(1)}, f32[3,64,512]{2,1,0:T(8,128)S(1)}, u32[]{:S(2)}, u32[]{:S(2)}) %collective-permute-start.6) | collective-permute-done | bytes 393248 | tf_op jit(solution)/shard_map/ppermute | solution.py:482
  61.8 1.8 %merge.1 = f32[4,64,512]{2,1,0:T(8,128)} custom-call(f32[8]{0:T(128)S(1)} %copy-done, f32[3,64,512]{2,1,0:T(8,128)S(1)} %collective-permute-done.4.refs_0_, f32[3,64,512]{2,1,0:T(8,128)S(1)} %collective-permute-done.5.refs_1_, f32[3,64,512]{2,1,0:T(8,128)S(1)} %collective-permute-done.6.refs_2_, f32[3,64,512]{2,1,0:T(8,128)S(1)} %shard_map.30.refs_3_), custom_call_target="tpu_custom_call" | custom-call | tf_op jit(solution)/shard_map/merge/pallas_call | solution.py:445
Async XLA Ops:
  0.0 7.3 %copy-start = (f32[8]{0:T(128)S(1)}, f32[8]{0:T(128)}, u32[]{:S(2)}) copy-start(f32[8]{0:T(128)} %transfer.11) | copy-start | bytes 100
  2.7 15.3 %collective-permute-start = (f32[1,64,2048]{2,1,0:T(8,128)}, f32[1,64,2048]{2,1,0:T(8,128)S(1)}, u32[]{:S(2)}, u32[]{:S(2)}) collective-permute-start(f32[1,64,2048]{2,1,0:T(8,128)} %get-tuple-element.12), channel_id=1, source_target_pairs={{0,8},{8,0},{16,24},{24,16},{1,9},{9,1},{17,25},{25,17},{2,10},{10... | collective-permute-start | bytes 1572872 | tf_op jit(solution)/shard_map/ppermute | solution.py:75
  5.8 12.1 %collective-permute-start.1 = (f32[1,64,2048]{2,1,0:T(8,128)}, f32[1,64,2048]{2,1,0:T(8,128)S(1)}, u32[]{:S(2)}, u32[]{:S(2)}) collective-permute-start(f32[1,64,2048]{2,1,0:T(8,128)} %get-tuple-element.13), channel_id=1, source_target_pairs={{8,16},{16,8},{9,17},{17,9},{10,18},{18,10},{11,19},{19,11},{12,20... | collective-permute-start | bytes 1572872 | tf_op jit(solution)/shard_map/ppermute | solution.py:75
  6.5 8.5 %collective-permute-start.2 = (f32[48,1,2048]{2,1,0:T(1,128)}, f32[48,1,2048]{2,1,0:T(1,128)S(1)}, u32[]{:S(2)}, u32[]{:S(2)}) collective-permute-start(f32[48,1,2048]{2,1,0:T(1,128)} %get-tuple-element.14), channel_id=1, source_target_pairs={{0,1},{1,0},{2,3},{3,2},{4,5},{5,4},{6,7},{7,6},{8,9},{9,8},{10,11... | collective-permute-start | bytes 1179656 | tf_op jit(solution)/shard_map/ppermute | solution.py:75
  6.6 8.5 %collective-permute-start.3 = (f32[48,1,2048]{2,1,0:T(1,128)}, f32[48,1,2048]{2,1,0:T(1,128)S(1)}, u32[]{:S(2)}, u32[]{:S(2)}) collective-permute-start(f32[48,1,2048]{2,1,0:T(1,128)} %get-tuple-element.15), channel_id=1, source_target_pairs={{1,2},{2,1},{3,4},{4,3},{5,6},{6,5},{9,10},{10,9},{11,12},{12,11},... | collective-permute-start | bytes 1179656 | tf_op jit(solution)/shard_map/ppermute | solution.py:75
  21.0 38.1 %collective-permute-start.4 = (f32[3,64,512]{2,1,0:T(8,128)S(1)}, f32[3,64,512]{2,1,0:T(8,128)S(1)}, u32[]{:S(2)}, u32[]{:S(2)}) collective-permute-start(f32[3,64,512]{2,1,0:T(8,128)S(1)} %get-tuple-element.18), channel_id=1, source_target_pairs={{0,16},{8,24},{16,0},{24,8},{1,17},{9,25},{17,1},{25,9},{2,18},{10... | collective-permute-start | bytes 1179656 | tf_op jit(solution)/shard_map/ppermute | solution.py:482
  36.5 22.6 %collective-permute-start.5 = (f32[3,64,512]{2,1,0:T(8,128)S(1)}, f32[3,64,512]{2,1,0:T(8,128)S(1)}, u32[]{:S(2)}, u32[]{:S(2)}) collective-permute-start(f32[3,64,512]{2,1,0:T(8,128)S(1)} %shard_map.28), channel_id=1, source_target_pairs={{0,8},{8,16},{16,24},{24,0},{1,9},{9,17},{17,25},{25,1},{2,10},{10... | collective-permute-start | bytes 1179656 | tf_op jit(solution)/shard_map/ppermute | solution.py:482
  46.0 15.8 %collective-permute-start.6 = (f32[3,64,512]{2,1,0:T(8,128)S(1)}, f32[3,64,512]{2,1,0:T(8,128)S(1)}, u32[]{:S(2)}, u32[]{:S(2)}) collective-permute-start(f32[3,64,512]{2,1,0:T(8,128)S(1)} %shard_map.29), channel_id=1, source_target_pairs={{0,24},{8,0},{16,8},{24,16},{1,25},{9,1},{17,9},{25,17},{2,26},{10... | collective-permute-start | bytes 1179656 | tf_op jit(solution)/shard_map/ppermute | solution.py:482

commit v2 on v0

--- a/solution.py
+++ b/solution.py
@@ -179,6 +179,13 @@
         pl.when(jnp.logical_not(self.has_left))(lambda: self.clear(0))
         pl.when(jnp.logical_not(self.has_right))(lambda: self.clear(self.chunks + 1))
 
+    def land_all(self):
+        for k in range(len(self.pieces)):
+            for c in range(1, self.chunks + 1):
+                self.copy(c, k).wait()
+            pl.when(self.has_left)(lambda k=k: self.copy(0, k).wait())
+            pl.when(self.has_right)(lambda k=k: self.copy(self.chunks + 1, k).wait())
+
     def land(self, c, k):
         @pl.when(c == 1)
         def _():
@@ -250,48 +257,45 @@
     return lax.fori_loop(0, trips, trip, carry)[0]
 
 
-def full_kernel(shift, tiles, pieces, total_slices, transfer, volume, *refs):
-    *halo, out, cells, sems, edge_sems = refs
+def full_kernel(shift, later, step, pieces, total_slices, transfer, volume, *refs):
     slices, rows, _ = volume.shape
+    halo, refs = refs[:4], refs[4:]
+    if later is None:
+        _, out, cells, edge_sems = refs
+    else:
+        _, _, out, cells, ahead, edge_sems, later_sems = refs
     chunks = out.shape[2] // LANES
-    trips = len(pieces)
-    groups = rows // SUBLANES // tiles
-    bricks = Bricks(volume, cells, sems, shift, chunks, pieces)
+    if later is not None:
+        following = Bricks(volume, ahead, later_sems, later, chunks, pieces)
+        following.start_all()
+    bricks = Bricks(volume, cells, None, shift, chunks, ())
     edges = Edges(bricks, edge_sems, *halo)
-    bricks.start_all()
     edges.start(range(1, chunks + 1))
     coef = coefficients(transfer, total_slices)
     ends = tile_constants()
+    at_rows = [SUBLANES * (t + 1) for t in range(rows // SUBLANES)]
 
     def group(index, carry):
-        c = index // groups + 1
-        row = pl.multiple_of((index % groups * tiles + 1) * SUBLANES, SUBLANES)
-        fresh = index % groups == 0
-
-        @pl.when(fresh)
-        def _():
-            edges.wait(c)
-            bricks.land(c, 0)
-
-        def arrive(k):
-            for part in range(1, trips):
-                pl.when(jnp.logical_and(fresh, k == part))(lambda part=part: bricks.land(c, part))
-
-        at_rows = [row + SUBLANES * t for t in range(tiles)]
-        states = march(cells, c, at_rows, 0, slices // trips, trips, coef, ends, arrive)
+        c = index + 1
+        edges.wait(c)
+        states = march(cells, c, at_rows, 0, step, slices // step, coef, ends, lambda k: None)
         for at_row, state in zip(at_rows, states):
             put(out, c, at_row, state)
         return carry
 
-    lax.fori_loop(0, chunks * groups, group, 0)
-
-
-def inner_kernel(shift, pieces, total_slices, transfer, volume, out, cells, sems):
+    lax.fori_loop(0, chunks, group, 0)
+    if later is not None:
+        following.land_all()
+
+
+def inner_kernel(shift, later, pieces, total_slices, transfer, volume, out, cells, ahead, sems, later_sems):
     slices, rows, _ = volume.shape
     chunks = out.shape[2] // LANES
     trips = len(pieces)
     bricks = Bricks(volume, cells, sems, shift, chunks, pieces)
     bricks.start_all()
+    following = Bricks(volume, ahead, later_sems, later, chunks, pieces)
+    following.start_all()
     coef = coefficients(transfer, total_slices)
     ends = tile_constants()
     at_rows = [SUBLANES * (t + 2) for t in range(rows // SUBLANES - 2)]
@@ -312,15 +316,15 @@
         return carry
 
     lax.fori_loop(0, chunks, group, 0)
-
-
-def rest_kernel(shift, pieces, total_slices, transfer, volume, *refs):
-    *halo, inner, out, cells, sems, edge_sems = refs
+    following.land_all()
+
+
+def rest_kernel(shift, total_slices, transfer, volume, *refs):
+    *halo, inner, _, out, cells, edge_sems = refs
     slices, rows, _ = volume.shape
     chunks = out.shape[2] // LANES
-    bricks = Bricks(volume, cells, sems, shift, chunks, pieces)
+    bricks = Bricks(volume, cells, None, shift, chunks, ())
     edges = Edges(bricks, edge_sems, *halo)
-    bricks.start_all()
     edges.start(range(1, chunks + 1))
     coef = coefficients(transfer, total_slices)
     ends = tile_constants()
@@ -328,8 +332,6 @@
     def group(index, carry):
         c = index + 1
         edges.wait(c)
-        for k in range(len(pieces)):
-            bricks.land(c, k)
         outer = [SUBLANES, rows]
         states = march(cells, c, outer, 0, slices, 1, coef, ends, lambda k: None)
         for at_row, state in zip(outer, states):
@@ -353,23 +355,26 @@
     lax.fori_loop(0, chunks, group, 0)
 
 
-def render(kernel, pieces, transfer, volume, extra, width, halo):
+def cells_shape(volume, width):
     slices, rows, _ = volume.shape
-    chunks = width // LANES
-    scratch = [
-        pltpu.VMEM((chunks + 2, slices + 2, rows + 2 * SUBLANES, LANES), jnp.float32),
-        pltpu.SemaphoreType.DMA((chunks + 2, len(pieces))),
-    ]
-    if halo:
-        scratch.append(pltpu.SemaphoreType.DMA((chunks + 1, 4)))
+    return (width // LANES + 2, slices + 2, rows + 2 * SUBLANES, LANES)
+
+
+def call(kernel, transfer, volume, halo, done, buffers, fresh, counts, width, limit=16):
+    shape = cells_shape(volume, width)
+    held = jax.ShapeDtypeStruct(shape, jnp.float32)
+    first = 2 + len(halo) + len(done)
+    scratch = [pltpu.SemaphoreType.DMA((shape[0], count)) for count in counts]
     return pl.pallas_call(
         kernel,
-        in_specs=[SMEM, ANY] + [ANY] * min(4, len(extra)) + [VMEM] * (len(extra) - 4),
-        out_specs=VMEM,
-        out_shape=jax.ShapeDtypeStruct((3, rows, width), jnp.float32),
+        in_specs=[SMEM, ANY] + [ANY] * len(halo) + [VMEM] * (len(done) + len(buffers)),
+        out_specs=[VMEM] * (1 + len(buffers) + fresh),
+        out_shape=[jax.ShapeDtypeStruct((3, volume.shape[1], width), jnp.float32)]
+        + [held] * (len(buffers) + fresh),
+        input_output_aliases={first + i: 1 + i for i in range(len(buffers))},
         scratch_shapes=scratch,
-        compiler_params=pltpu.CompilerParams(vmem_limit_bytes=32 << 20),
-    )(transfer, volume, *extra)
+        compiler_params=pltpu.CompilerParams(vmem_limit_bytes=limit << 20),
+    )(transfer, volume, *halo, *done, *buffers)
 
 
 def merge_kernel(shifts, transfer, *refs):
@@ -426,31 +431,27 @@
     total_slices = slices * groups
     width = columns // groups
     slab_a, slab_b, strip_a, strip_b = cut(volume)
-    edges = (
-        swap(slab_a, "depth", 0),
-        swap(slab_b, "depth", 1),
-        swap(strip_a, "row", 0),
-        swap(strip_b, "row", 1),
-    )
+    edges = (swap(slab_a, "depth", 0), swap(slab_b, "depth", 1), swap(strip_a, "row", 0), swap(strip_b, "row", 1))
     half = slices // 2
     halves = [(0, half + 1, 0, rows), (half + 1, slices - half - 1, 0, rows)]
-    ring = [
-        (0, slices, 0, 2 * SUBLANES),
-        (0, slices, rows - 2 * SUBLANES, 2 * SUBLANES),
-        (0, 2, 2 * SUBLANES, rows - 4 * SUBLANES),
-        (slices - 2, 2, 2 * SUBLANES, rows - 4 * SUBLANES),
-    ]
     shifts = order_of_shifts(groups)
     parts = []
+    counts = (4, len(halves))
     for stage, shift in enumerate(shifts):
+        later = shifts[stage + 1] if shift else None
         if stage == 0:
-            kernel = functools.partial(inner_kernel, shift, halves, total_slices)
-            inner = render(kernel, halves, transfer, volume, (), width, False)
-            kernel = functools.partial(rest_kernel, shift, ring, total_slices)
-            part = render(kernel, ring, transfer, volume, edges + (inner,), width, True)
+            kernel = functools.partial(inner_kernel, shift, later, halves, total_slices)
+            pair = (len(halves), len(halves))
+            inner, cells, ahead = call(kernel, transfer, volume, (), (), (), 2, pair, width)
+            kernel = functools.partial(rest_kernel, shift, total_slices)
+            part, free = call(kernel, transfer, volume, edges, (inner,), (cells,), 0, (4,), width)
+        elif shift:
+            kernel = functools.partial(full_kernel, shift, later, half, halves, total_slices)
+            buffers = (ahead, free)
+            part, free, ahead = call(kernel, transfer, volume, edges, (), buffers, 0, counts, width)
         else:
-            kernel = functools.partial(full_kernel, shift, 8, halves, total_slices)
-            part = render(kernel, halves, transfer, volume, edges, width, True)
+            kernel = functools.partial(full_kernel, shift, None, half, halves, total_slices)
+            part, _ = call(kernel, transfer, volume, edges, (), (ahead,), 0, (4,), width, 28)
         if shift:
             pairs = [(i, (i + shift) % groups) for i in range(groups)]
             part = lax.ppermute(part, "depth", pairs)
@@ -466,6 +467,4 @@
     in_specs = (P("depth", "row", None), P())
     out_specs = P(None, "row", "depth")
 
-    return jax.shard_map(
-        on_device, mesh=mesh, in_specs=in_specs, out_specs=out_specs, check_vma=False
-    )
+    return jax.shard_map(on_device, mesh=mesh, in_specs=in_specs, out_specs=out_specs, check_vma=False)

time: 72.7 us -> 63.8 us (0.88)
  waiting for transfers between devices: 15.4 us -> 7.54 us
  Pallas kernels: 44.9 us -> 41.5 us
  starting transfers between devices: 12.2 us -> 14.5 us
    ppermute x3, waiting for transfers between devices: 12.4 us -> 4.76 us  [on_device(): part = lax.ppermute(part, 'depth', pairs)]
    pallas_call x5, Pallas kernels: 40.4 us -> 37 us  [call(): pl.pallas_call(kernel, in_specs=[SMEM, ANY] + [ANY] * len(halo) + [VMEM]...]
    ppermute x3, starting transfers between devices: 7.6 us -> 9.91 us  [on_device(): part = lax.ppermute(part, 'depth', pairs)]
  transfers between devices with their start and end apart: 7 -> 7, of which waited for: 2 -> 2; matrix products, arithmetic and copies ran while one was open for 0% -> 0% of each run, Pallas kernels for 43% -> 53%
where the time goes in v2:
time: 63.8 us; the launch traced here: 63.6 us
  Pallas kernels  41.5 us (65%)
  starting transfers between devices  14.5 us (23%)
  waiting for transfers between devices  7.54 us (12%)
    pallas_call x5, Pallas kernels, call(): pl.pallas_call(kernel, in_specs=[SMEM, ANY] + [ANY] * len(halo) + [VMEM]...  37 us
    ppermute x3, starting transfers between devices, on_device(): part = lax.ppermute(part, 'depth', pairs)  9.91 us
    ppermute x3, waiting for transfers between devices, on_device(): part = lax.ppermute(part, 'depth', pairs)  4.76 us
    ppermute x4, starting transfers between devices, swap(): return lax.ppermute(value, axis, pairs)  4.56 us
    ppermute x4, waiting for transfers between devices, swap(): return lax.ppermute(value, axis, pairs)  2.77 us
    pallas_call x1, Pallas kernels, cut(): pl.pallas_call(cut_kernel, in_specs=[ANY], out_specs=[VMEM] * 4, out_shap...  2.72 us
    pallas_call x1, Pallas kernels, merge(): pl.pallas_call(functools.partial(merge_kernel, shifts), in_specs=[SMEM] +...  1.75 us
  transfers between devices with their start and end apart: 7, of which 2 were waited for; matrix products, arithmetic and copies ran while one was open for 0% of the time, Pallas kernels for 53%

profile of v2, /device:TPU:0, one launch (start us, length us, event | category | flops | bytes accessed | tf_op | source)
XLA Modules:
  0.0 63.6 jit_solution(8814781931161492236)
XLA Ops:
  0.0 0.0 copy-start
  0.0 2.7 %cut.1 = (f32[1,64,2048]{2,1,0:T(8,128)}, f32[1,64,2048]{2,1,0:T(8,128)}, f32[48,1,2048]{2,1,0:T(1,128)}, f32[48,1,2048]{2,1,0:T(1,128)}) custom-call(f32[48,64,2048]{2,1,0:T(8,128)} %volume.11), custom_call_target="tpu_custom_call" | custom-call | tf_op jit(solution)/shard_map/cut/pallas_call | solution.py:61
  2.7 3.1 %collective-permute-start = (f32[1,64,2048]{2,1,0:T(8,128)}, f32[1,64,2048]{2,1,0:T(8,128)S(1)}, u32[]{:S(2)}, u32[]{:S(2)}) collective-permute-start(f32[1,64,2048]{2,1,0:T(8,128)} %get-tuple-element.20), channel_id=1, source_target_pairs={{0,8},{8,0},{16,24},{24,16},{1,9},{9,1},{17,25},{25,17},{2,10},{10... | collective-permute-start | bytes 1572872 | tf_op jit(solution)/shard_map/ppermute | solution.py:75
  5.9 0.7 %collective-permute-start.1 = (f32[1,64,2048]{2,1,0:T(8,128)}, f32[1,64,2048]{2,1,0:T(8,128)S(1)}, u32[]{:S(2)}, u32[]{:S(2)}) collective-permute-start(f32[1,64,2048]{2,1,0:T(8,128)} %get-tuple-element.21), channel_id=1, source_target_pairs={{8,16},{16,8},{9,17},{17,9},{10,18},{18,10},{11,19},{19,11},{12,20... | collective-permute-start | bytes 1572872 | tf_op jit(solution)/shard_map/ppermute | solution.py:75
  6.5 0.1 collective-permute-start.2
  6.6 0.7 %collective-permute-start.3 = (f32[48,1,2048]{2,1,0:T(1,128)}, f32[48,1,2048]{2,1,0:T(1,128)S(1)}, u32[]{:S(2)}, u32[]{:S(2)}) collective-permute-start(f32[48,1,2048]{2,1,0:T(1,128)} %get-tuple-element.23), channel_id=1, source_target_pairs={{1,2},{2,1},{3,4},{4,3},{5,6},{6,5},{9,10},{10,9},{11,12},{12,11},... | collective-permute-start | bytes 1179656 | tf_op jit(solution)/shard_map/ppermute | solution.py:75
  7.3 0.0 copy-done
  7.3 7.9 %shard_map.28 = (f32[3,64,512]{2,1,0:T(8,128)S(1)}, f32[6,50,80,128]{3,2,1,0:T(8,128)S(1)}, f32[6,50,80,128]{3,2,1,0:T(8,128)S(1)}) custom-call(f32[8]{0:T(128)S(1)} %copy-done, f32[48,64,2048]{2,1,0:T(8,128)} %volume.11), custom_call_target="tpu_custom_call" | custom-call | tf_op jit(solution)/shard_map/pallas_call | solution.py:368
  15.2 0.0 collective-permute-done.2.refs_2_
  15.2 0.0 collective-permute-done.3.refs_3_
  15.2 2.8 %collective-permute-done.refs_0_ = f32[1,64,2048]{2,1,0:T(8,128)S(1)} collective-permute-done((f32[1,64,2048]{2,1,0:T(8,128)}, f32[1,64,2048]{2,1,0:T(8,128)S(1)}, u32[]{:S(2)}, u32[]{:S(2)}) %collective-permute-start) | collective-permute-done | bytes 524320 | tf_op jit(solution)/shard_map/ppermute | solution.py:75
  18.0 0.0 collective-permute-done.1.refs_1_
  18.0 3.1 %shard_map.29 = (f32[3,64,512]{2,1,0:T(8,128)S(1)}, f32[6,50,80,128]{3,2,1,0:T(8,128)S(1)}) custom-call(f32[8]{0:T(128)S(1)} %copy-done, f32[48,64,2048]{2,1,0:T(8,128)} %volume.11, f32[1,64,2048]{2,1,0:T(8,128)S(1)} %collective-permute-done.refs_0_, f32[1,64,2048]{2,1,0:T(8,128)S(1)} %collective-permute-done.1.refs_1_, ...), custom_call_target="tpu_custom_call", output_to_operand_aliasing={{1}: (7, {})} | custom-call | tf_op jit(solution)/shard_map/pallas_call | solution.py:368
  21.1 6.0 %collective-permute-start.4 = (f32[3,64,512]{2,1,0:T(8,128)S(1)}, f32[3,64,512]{2,1,0:T(8,128)S(1)}, u32[]{:S(2)}, u32[]{:S(2)}) collective-permute-start(f32[3,64,512]{2,1,0:T(8,128)S(1)} %get-tuple-element.26), channel_id=1, source_target_pairs={{0,16},{8,24},{16,0},{24,8},{1,17},{9,25},{17,1},{25,9},{2,18},{10... | collective-permute-start | bytes 1179656 | tf_op jit(solution)/shard_map/ppermute | solution.py:457
  27.1 8.8 %shard_map.30 = (f32[3,64,512]{2,1,0:T(8,128)S(1)}, f32[6,50,80,128]{3,2,1,0:T(8,128)S(1)}, f32[6,50,80,128]{3,2,1,0:T(8,128)S(1)}) custom-call(f32[8]{0:T(128)S(1)} %copy-done, f32[48,64,2048]{2,1,0:T(8,128)} %volume.11, f32[1,64,2048]{2,1,0:T(8,128)S(1)} %collective-permute-done.refs_0_, ...), custom_call_target="tpu_custom_call", output_to_operand_aliasing={{1}: (6, {}), {2}: (7, {})} | custom-call | tf_op jit(solution)/shard_map/pallas_call | solution.py:368
  35.9 0.1 collective-permute-start.5
  36.0 8.8 %shard_map.31 = (f32[3,64,512]{2,1,0:T(8,128)S(1)}, f32[6,50,80,128]{3,2,1,0:T(8,128)S(1)}, f32[6,50,80,128]{3,2,1,0:T(8,128)S(1)}) custom-call(f32[8]{0:T(128)S(1)} %copy-done, f32[48,64,2048]{2,1,0:T(8,128)} %volume.11, f32[1,64,2048]{2,1,0:T(8,128)S(1)} %collective-permute-done.refs_0_, ...), custom_call_target="tpu_custom_call", output_to_operand_aliasing={{1}: (6, {}), {2}: (7, {})} | custom-call | tf_op jit(solution)/shard_map/pallas_call | solution.py:368
  44.8 3.9 %collective-permute-start.6 = (f32[3,64,512]{2,1,0:T(8,128)S(1)}, f32[3,64,512]{2,1,0:T(8,128)S(1)}, u32[]{:S(2)}, u32[]{:S(2)}) collective-permute-start(f32[3,64,512]{2,1,0:T(8,128)S(1)} %get-tuple-element.32), channel_id=1, source_target_pairs={{0,24},{8,0},{16,8},{24,16},{1,25},{9,1},{17,9},{25,17},{2,26},{10... | collective-permute-start | bytes 1179656 | tf_op jit(solution)/shard_map/ppermute | solution.py:457
  48.7 8.4 %shard_map.32 = (f32[3,64,512]{2,1,0:T(8,128)S(1)}, f32[6,50,80,128]{3,2,1,0:T(8,128)S(1)}) custom-call(f32[8]{0:T(128)S(1)} %copy-done, f32[48,64,2048]{2,1,0:T(8,128)} %volume.11, f32[1,64,2048]{2,1,0:T(8,128)S(1)} %collective-permute-done.refs_0_, f32[1,64,2048]{2,1,0:T(8,128)S(1)} %collective-permute-done.1.refs_1_, ...), custom_call_target="tpu_custom_call", output_to_operand_aliasing={{1}: (6, {})} | custom-call | tf_op jit(solution)/shard_map/pallas_call | solution.py:368
  57.1 0.0 collective-permute-done.4.refs_0_
  57.1 0.0 collective-permute-done.5.refs_1_
  57.1 4.8 %collective-permute-done.6.refs_2_ = f32[3,64,512]{2,1,0:T(8,128)S(1)} collective-permute-done((f32[3,64,512]{2,1,0:T(8,128)S(1)}, f32[3,64,512]{2,1,0:T(8,128)S(1)}, u32[]{:S(2)}, u32[]{:S(2)}) %collective-permute-start.6) | collective-permute-done | bytes 393248 | tf_op jit(solution)/shard_map/ppermute | solution.py:457
  61.8 1.8 %merge.1 = f32[4,64,512]{2,1,0:T(8,128)} custom-call(f32[8]{0:T(128)S(1)} %copy-done, f32[3,64,512]{2,1,0:T(8,128)S(1)} %collective-permute-done.4.refs_0_, f32[3,64,512]{2,1,0:T(8,128)S(1)} %collective-permute-done.5.refs_1_, f32[3,64,512]{2,1,0:T(8,128)S(1)} %collective-permute-done.6.refs_2_, f32[3,64,512]{2,1,0:T(8,128)S(1)} %get-tuple-element.34.refs_3_), custom_call_target="tpu_custom_call" | custom-call | tf_op jit(solution)/shard_map/merge/pallas_call | solution.py:418
Async XLA Ops:
  0.0 7.3 %copy-start = (f32[8]{0:T(128)S(1)}, f32[8]{0:T(128)}, u32[]{:S(2)}) copy-start(f32[8]{0:T(128)} %transfer.11) | copy-start | bytes 100
  2.7 15.3 %collective-permute-start = (f32[1,64,2048]{2,1,0:T(8,128)}, f32[1,64,2048]{2,1,0:T(8,128)S(1)}, u32[]{:S(2)}, u32[]{:S(2)}) collective-permute-start(f32[1,64,2048]{2,1,0:T(8,128)} %get-tuple-element.20), channel_id=1, source_target_pairs={{0,8},{8,0},{16,24},{24,16},{1,9},{9,1},{17,25},{25,17},{2,10},{10... | collective-permute-start | bytes 1572872 | tf_op jit(solution)/shard_map/ppermute | solution.py:75
  5.9 12.1 %collective-permute-start.1 = (f32[1,64,2048]{2,1,0:T(8,128)}, f32[1,64,2048]{2,1,0:T(8,128)S(1)}, u32[]{:S(2)}, u32[]{:S(2)}) collective-permute-start(f32[1,64,2048]{2,1,0:T(8,128)} %get-tuple-element.21), channel_id=1, source_target_pairs={{8,16},{16,8},{9,17},{17,9},{10,18},{18,10},{11,19},{19,11},{12,20... | collective-permute-start | bytes 1572872 | tf_op jit(solution)/shard_map/ppermute | solution.py:75
  6.5 8.7 %collective-permute-start.2 = (f32[48,1,2048]{2,1,0:T(1,128)}, f32[48,1,2048]{2,1,0:T(1,128)S(1)}, u32[]{:S(2)}, u32[]{:S(2)}) collective-permute-start(f32[48,1,2048]{2,1,0:T(1,128)} %get-tuple-element.22), channel_id=1, source_target_pairs={{0,1},{1,0},{2,3},{3,2},{4,5},{5,4},{6,7},{7,6},{8,9},{9,8},{10,11... | collective-permute-start | bytes 1179656 | tf_op jit(solution)/shard_map/ppermute | solution.py:75
  6.6 8.6 %collective-permute-start.3 = (f32[48,1,2048]{2,1,0:T(1,128)}, f32[48,1,2048]{2,1,0:T(1,128)S(1)}, u32[]{:S(2)}, u32[]{:S(2)}) collective-permute-start(f32[48,1,2048]{2,1,0:T(1,128)} %get-tuple-element.23), channel_id=1, source_target_pairs={{1,2},{2,1},{3,4},{4,3},{5,6},{6,5},{9,10},{10,9},{11,12},{12,11},... | collective-permute-start | bytes 1179656 | tf_op jit(solution)/shard_map/ppermute | solution.py:75
  21.1 36.0 %collective-permute-start.4 = (f32[3,64,512]{2,1,0:T(8,128)S(1)}, f32[3,64,512]{2,1,0:T(8,128)S(1)}, u32[]{:S(2)}, u32[]{:S(2)}) collective-permute-start(f32[3,64,512]{2,1,0:T(8,128)S(1)} %get-tuple-element.26), channel_id=1, source_target_pairs={{0,16},{8,24},{16,0},{24,8},{1,17},{9,25},{17,1},{25,9},{2,18},{10... | collective-permute-start | bytes 1179656 | tf_op jit(solution)/shard_map/ppermute | solution.py:457
  35.9 21.2 %collective-permute-start.5 = (f32[3,64,512]{2,1,0:T(8,128)S(1)}, f32[3,64,512]{2,1,0:T(8,128)S(1)}, u32[]{:S(2)}, u32[]{:S(2)}) collective-permute-start(f32[3,64,512]{2,1,0:T(8,128)S(1)} %get-tuple-element.29), channel_id=1, source_target_pairs={{0,8},{8,16},{16,24},{24,0},{1,9},{9,17},{17,25},{25,1},{2,10},{10... | collective-permute-start | bytes 1179656 | tf_op jit(solution)/shard_map/ppermute | solution.py:457
  44.8 17.0 %collective-permute-start.6 = (f32[3,64,512]{2,1,0:T(8,128)S(1)}, f32[3,64,512]{2,1,0:T(8,128)S(1)}, u32[]{:S(2)}, u32[]{:S(2)}) collective-permute-start(f32[3,64,512]{2,1,0:T(8,128)S(1)} %get-tuple-element.32), channel_id=1, source_target_pairs={{0,24},{8,0},{16,8},{24,16},{1,25},{9,1},{17,9},{25,17},{2,26},{10... | collective-permute-start | bytes 1179656 | tf_op jit(solution)/shard_map/ppermute | solution.py:457
